TPU v7x, 256 devices: a whole 4x4x8 slice. The times are simulated.
256 devices in a mesh: row: 16 (over y, z_lo), col: 8 (over x, core), tp: 2 (over z_hi).
Axes of the slice: x: 4, y: 4, z: 8 (z_hi: 2, z_lo: 4; z = z_hi * 4 + z_lo), core: 2. Of those that a mesh axis runs over, the one named last changes fastest.
Arguments:
- gram: float32 [8, 16, 128, 1, 8, 2048], P(None, 'row', 'tp', None, 'col'), may hold values from -24 to 24
- inv_factor: bfloat16 [1024, 1024], replicated, as said below
- cross_gram: bfloat16 [8, 16, 128, 1024], P(None, 'row', 'tp'), may hold values from -24 to 24
- down_rows: bfloat16 [29568, 4096], P(('row', 'tp'), 'col'), may hold values from -0.03125 to 0.03125
- removed: int32 [1024], replicated, may hold values from 0 to 29567, as said below
Outputs:
- updated: float32 [8, 16, 128, 1, 8, 2048], P(None, 'row', 'tp', None, 'col')
- rhs_next: float32 [8, 16, 128, 4096], P(None, 'row', 'tp', 'col')
Inputs may be any that keep to these rules, and one draw needn't show every extreme that they name: `inv_factor`: zero above the diagonal. `removed`: distinct ids in ascending order; among the neurons s * 924 to (s + 1) * 924 - 1 of any shard s at most 128 are listed, and one shard holds exactly 128.
All inputs are finite; a program needn't handle non-finite values.
Results may differ from a plain program's by a relative error of at most 0.0003.
Values may be sent and summed in bfloat16 or wider, within the bound.
A program may use at most 128 MiB of HBM per device.

v0:
```python
import jax
import jax.numpy as jnp
from jax import lax
from jax.sharding import PartitionSpec as P


def broadcast(block, axis, holder):
    block = jnp.where(lax.axis_index(axis) == holder, block, jnp.zeros_like(block))
    return lax.psum(block, axis)


def per_device(gram, inv_factor, cross_gram, down_rows, removed):
    highest = lax.Precision.HIGHEST
    cycles = gram.shape[0]
    half = gram.shape[2]
    col_cycles = gram.shape[3]
    block = gram.shape[5]
    rows_local = cycles * half
    panel_width = inv_factor.shape[0]
    grid = gram.reshape(rows_local, col_cycles, block)
    factor = inv_factor.astype(jnp.float32)
    head_columns = grid[:, 0, :panel_width]
    panel = broadcast(head_columns, "col", 0)
    left = jnp.dot(panel, factor.T, precision=highest, preferred_element_type=jnp.float32)
    col_count = lax.axis_size("col")
    by_cycle = left.reshape(col_cycles, col_count, half, panel_width)
    wanted = lax.dynamic_index_in_dim(by_cycle, lax.axis_index("col"), axis=1, keepdims=False)
    product = jnp.einsum(
        "rp,cwp->rcw",
        left,
        lax.all_gather(wanted, ("row", "tp"), axis=1, tiled=True),
        precision=highest,
        preferred_element_type=jnp.float32,
    )
    updated = grid - product
    shard = down_rows.shape[0]
    count_all = removed.shape[0]
    member = lax.axis_index(("row", "tp"))
    owner = removed // shard
    capacity = 4 * count_all // lax.axis_size(("row", "tp"))
    earlier = jnp.sum(owner[None, :] < owner[:, None], axis=1)
    within = jnp.arange(count_all, dtype=jnp.int32) - earlier
    own_start = jnp.sum(owner < member)
    slot_ids = jnp.clip(own_start + jnp.arange(capacity, dtype=jnp.int32), 0, count_all - 1)
    local_ids = jnp.clip(removed[slot_ids] - member * shard, 0, shard - 1)
    packed = jnp.take(down_rows, local_ids, axis=0)
    everyone = lax.all_gather(packed, ("row", "tp"), axis=0, tiled=True)
    lost_rows = jnp.take(everyone, owner * capacity + within, axis=0)
    cross = cross_gram.reshape(rows_local, cross_gram.shape[3])
    rhs = jnp.dot(cross, lost_rows, preferred_element_type=jnp.float32)
    leading = rhs[:half]
    stacked = lax.all_gather(leading, ("row", "tp"), axis=0, tiled=True)
    solved = jnp.dot(
        factor, stacked[:panel_width], precision=highest, preferred_element_type=jnp.float32
    )
    rhs_next = rhs - jnp.dot(left, solved, precision=highest, preferred_element_type=jnp.float32)
    return (updated.reshape(gram.shape), rhs_next.reshape(cycles, 1, half, rhs.shape[1]))


def solution(mesh):
    return jax.shard_map(
        per_device,
        mesh=mesh,
        in_specs=(
            P(None, "row", "tp", None, "col", None),
            P(),
            P(None, "row", "tp", None),
            P(("row", "tp"), "col"),
            P(),
        ),
        out_specs=(P(None, "row", "tp", None, "col", None), P(None, "row", "tp", "col")),
        check_vma=False,
    )
```

profile of v0, /device:TPU:24, one launch (start us, length us, event | category | flops | bytes accessed | tf_op | source)
XLA Modules:
  0.0 1071.5 jit_solution(9700904976470419357)
XLA Ops:
  8.0 0.0 copy-start
  8.0 0.0 all-gather.5.cloned.1.call-start
  8.1 1.5 convert_reduce_fusion.1
  9.5 0.7 fusion.10
  10.2 1.6 gather_fusion
  11.9 2.2 gather_fusion.1
  14.1 0.7 broadcast_select_fusion.1
  14.8 0.0 all-gather.5.cloned.1.call-update
  14.8 0.0 all-reduce.2.cloned.1.call-start
  14.9 3.4 broadcast_select_fusion
  18.3 1.8 copy.16
  20.1 0.0 all-reduce.2.cloned.1.call-update
  20.1 0.0 all-gather.7.cloned.1.call-start
  20.1 0.6 convert_reduce_fusion
  20.7 264.1 %all-gather.5.cloned.1.call-done = bf16[4096,512]{1,0:T(8,128)(2,1)} async-done(((bf16[128,512]{1,0:T(8,128)(2,1)}), bf16[4096,512]{1,0:T(8,128)(2,1)}) %all-gather.5.cloned.1.call-update) | async-done | bytes 4194320 | tf_op jit(solution)/shard_map/all_gather | solution.py:47
  284.8 7.8 gather_fusion.2
  292.7 2.3 convolution_bitcast_fusion
  295.0 0.7 slice.19
  295.6 0.0 all-gather.7.cloned.1.call-update
  295.7 0.2 all-gather.9.cloned.1.call-start
  295.9 0.0 all-reduce.2.cloned.1.call-done
  295.9 0.0 copy-done
  295.9 5.1 fusion.13
  301.0 0.0 copy-start.1
  301.0 1.3 copy-done.1
  302.3 0.7 constant_dynamic-slice_fusion
  303.1 0.0 all-gather.9.cloned.1.call-update
  303.1 6.2 copy.13
  309.3 257.5 %all-gather.7.cloned.1.call-done = f32[2048,512]{1,0:T(8,128)} async-done(((f32[64,512]{1,0:T(8,128)}), f32[2048,512]{1,0:T(8,128)}) %all-gather.7.cloned.1.call-update) | async-done | bytes 4194320 | tf_op jit(solution)/shard_map/all_gather | solution.py:52
  566.7 0.0 copy-start.2
  566.7 8.7 fusion.4
  575.4 0.0 copy-done.2
  575.4 4.5 convolution_subtract_fusion
  579.9 461.2 %all-gather.9.cloned.1.call-done = f32[1,1,2048,1024]{3,2,1,0:T(8,128)} async-done(((f32[1,1,64,1024]{3,2,1,0:T(8,128)}), f32[1,1,2048,1024]{3,2,1,0:T(8,128)}) %all-gather.9.cloned.1.call-update) | async-done | bytes 8388624 | tf_op jit(solution)/shard_map/all_gather | solution.py:31
  1041.1 16.9 %bitcast_subtract_fusion = f32[512,2048]{1,0:T(8,128)S(1)} fusion(f32[8,1,64,1,1,2048]{5,2,3,4,1,0:T(8,128)} %copy.13, f32[512,1024]{1,0:T(8,128)} %copy-done.1, f32[1,1,2048,1024]{3,2,1,0:T(8,128)} %all-gather.9.cloned.1.call-done), kind=kOutput, calls=%fused_computation.5 | convolution fusion | flops 12885950464 | bytes 18874368 | tf_op jit(solution)/shard_map/rp,cwp->rcw/dot_general | solution.py:28
  1058.0 6.3 copy.11
  (6 shorter events, 0.1 us)
Async XLA Ops:
  8.0 287.9 %copy-start = (bf16[1024,1024]{1,0:T(8,128)(2,1)S(1)}, bf16[1024,1024]{1,0:T(8,128)(2,1)}, u32[]{:S(2)}) copy-start(bf16[1024,1024]{1,0:T(8,128)(2,1)} %param.6) | copy-start | bytes 6291460
  8.0 276.8 %all-gather.5.cloned.1.call-start = ((), (), s32[]{:S(2)}) async-start(), calls=%async_computation.1 | async-start | bytes 4325376 | tf_op jit(solution)/shard_map/all_gather | solution.py:47
  14.8 281.1 %all-reduce.2.cloned.1.call-start = ((), (), s32[]{:S(2)}) async-start(), calls=%async_computation | async-start | bytes 4194304 | tf_op jit(solution)/shard_map/psum | solution.py:9
  20.1 546.6 %all-gather.7.cloned.1.call-start = ((), (), s32[]{:S(2)}) async-start(), calls=%async_computation.2 | async-start | bytes 4325376 | tf_op jit(solution)/shard_map/all_gather | solution.py:52
  295.7 745.5 %all-gather.9.cloned.1.call-start = ((), (), s32[]{:S(2)}) async-start(), calls=%async_computation.3 | async-start | bytes 8650752 | tf_op jit(solution)/shard_map/all_gather | solution.py:31
  301.0 1.3 copy-start.1
  566.7 8.7 copy-start.2
Sparse Core Ops, SparseCore 0:
  14.9 269.8 all-gather.4
  295.8 270.8 all-gather.6
  568.5 472.5 all-gather.8
Sparse Core Ops, SparseCore 1:
  20.2 75.2 all-reduce.1
where the time goes:
time: 1070 us
  waiting for transfers between devices  983 us (92%)
  matrix products  37.4 us (3%)
  local copies, waits for them, and re-layouts  28.6 us (3%)
  between operations  15.3 us (1%)
    all_gather x1, waiting for transfers between devices, per_device(): lax.all_gather(wanted, ('row', 'tp'), axis=1, tiled=True)  461 us
    all_gather x1, waiting for transfers between devices, per_device(): everyone = lax.all_gather(packed, ('row', 'tp'), axis=0, tiled=True)  264 us
    all_gather x1, waiting for transfers between devices, per_device(): stacked = lax.all_gather(leading, ('row', 'tp'), axis=0, tiled=True)  257 us
  transfers between devices with their start and end apart: 4, of which 3 were waited for; matrix products, arithmetic and copies ran while one was open for 4% of the time, Pallas kernels for 0%

commit v1 on v0

--- a/solution.py
+++ b/solution.py
@@ -2,6 +2,7 @@
 import jax.numpy as jnp
 from jax import lax
 from jax.sharding import PartitionSpec as P
+from jax.lax import all_to_all, axis_size
 
 
 def broadcast(block, axis, holder):
@@ -49,7 +50,9 @@
     cross = cross_gram.reshape(rows_local, cross_gram.shape[3])
     rhs = jnp.dot(cross, lost_rows, preferred_element_type=jnp.float32)
     leading = rhs[:half]
-    stacked = lax.all_gather(leading, ("row", "tp"), axis=0, tiled=True)
+    stacked = jnp.concatenate(
+        all_to_all(jnp.stack(axis_size(("row", "tp")) * [leading]), ("row", "tp"), 0, 0), axis=0
+    )
     solved = jnp.dot(
         factor, stacked[:panel_width], precision=highest, preferred_element_type=jnp.float32
     )

time: 1070 us -> 863 us (0.81)
  waiting for transfers between devices: 983 us -> 759 us
    all_gather x1 -> x0, waiting for transfers between devices: 257 us -> none  [per_device(): stacked = lax.all_gather(leading, ('row', 'tp'), axis=0, tiled=True)]
    all_to_all x0 -> x1, waiting for transfers between devices: none -> 110 us  [per_device(): all_to_all(jnp.stack(axis_size(('row', 'tp')) * [leading]), ('row', 'tp')...]
    all_gather x1, waiting for transfers between devices: 461 us -> 386 us  [per_device(): lax.all_gather(wanted, ('row', 'tp'), axis=1, tiled=True)]
    all_gather x1, waiting for transfers between devices: 264 us -> 192 us  [per_device(): everyone = lax.all_gather(packed, ('row', 'tp'), axis=0, tiled=True)]
    psum x1, waiting for transfers between devices: 0.03 us -> 71 us  [broadcast(): return lax.psum(block, axis)]
  transfers between devices with their start and end apart: 4 -> 4, of which waited for: 3 -> 4; matrix products, arithmetic and copies ran while one was open for 4% -> 5% of each run, Pallas kernels for 0% -> 0%
where the time goes in v1:
time: 863 us; the launch traced here: 857 us
  waiting for transfers between devices  759 us (88%)
  matrix products  35.8 us (4%)
  local copies, waits for them, and re-layouts  30.8 us (4%)
  between operations  15.6 us (2%)
  starting transfers between devices  9.74 us (1%)
    all_gather x1, waiting for transfers between devices, per_device(): lax.all_gather(wanted, ('row', 'tp'), axis=1, tiled=True)  386 us
    all_gather x1, waiting for transfers between devices, per_device(): everyone = lax.all_gather(packed, ('row', 'tp'), axis=0, tiled=True)  192 us
    all_to_all x1, waiting for transfers between devices, per_device(): all_to_all(jnp.stack(axis_size(('row', 'tp')) * [leading]), ('row', 'tp')...  110 us
    psum x1, waiting for transfers between devices, broadcast(): return lax.psum(block, axis)  71 us
  transfers between devices with their start and end apart: 4, of which 4 were waited for; matrix products, arithmetic and copies ran while one was open for 5% of the time, Pallas kernels for 0%

profile of v1, /device:TPU:24, one launch (start us, length us, event | category | flops | bytes accessed | tf_op | source)
XLA Modules:
  0.0 857.2 jit_solution(5615983317136409368)
XLA Ops:
  8.0 0.0 copy-start
  8.0 0.0 all-reduce.2.cloned.1.call-start
  8.1 3.5 broadcast_select_fusion
  11.6 1.8 copy.16
  13.4 0.0 copy-start.1
  13.4 0.0 copy-start.4
  13.4 0.0 all-reduce.2.cloned.1.call-update
  13.4 0.0 all-gather.4.cloned.1.call-start
  13.5 0.6 copy-done.1
  14.1 0.6 convert_reduce_fusion.1
  14.7 0.7 fusion.8
  15.4 1.0 gather_fusion
  16.4 0.0 copy-done.4
  16.4 0.8 gather_fusion.1
  17.3 0.7 broadcast_select_fusion.1
  18.0 0.0 all-gather.4.cloned.1.call-update
  18.0 0.0 all-gather.6.cloned.1.call-start
  18.1 71.0 %all-reduce.2.cloned.1.call-done = f32[512,1024]{1,0:T(8,128)} async-done(((f32[512,1024]{1,0:T(8,128)}), f32[512,1024]{1,0:T(8,128)}) %all-reduce.2.cloned.1.call-update) | async-done | bytes 2097168 | tf_op jit(solution)/shard_map/psum | solution.py:10
  89.1 0.0 copy-done
  89.1 5.1 fusion.11
  94.1 0.0 copy-start.2
  94.1 1.3 copy-done.2
  95.5 0.7 constant_dynamic-slice_fusion
  96.2 0.0 all-gather.6.cloned.1.call-update
  96.2 0.6 convert_reduce_fusion
  96.8 191.8 %all-gather.4.cloned.1.call-done = bf16[4096,512]{1,0:T(8,128)(2,1)} async-done(((bf16[128,512]{1,0:T(8,128)(2,1)}), bf16[4096,512]{1,0:T(8,128)(2,1)}) %all-gather.4.cloned.1.call-update) | async-done | bytes 4194320 | tf_op jit(solution)/shard_map/all_gather | solution.py:48
  288.6 7.8 gather_fusion.2
  296.5 2.3 convolution_bitcast_fusion
  298.8 2.5 stack.2
  301.3 9.6 %all-to-all-start = ((f32[32,64,512]{2,1,0:T(8,128)}), f32[32,64,512]{2,1,0:T(8,128)}, u32[]{:S(2)}, u32[]{:S(2)}) async-start(f32[32,64,512]{2,1,0:T(8,128)} %stack.2), calls=%async_computation | async-start | bytes 8388608 | tf_op jit(solution)/shard_map/all_to_all | solution.py:54
  310.9 6.2 copy.13
  317.0 109.9 %all-to-all-done = f32[32,64,512]{2,1,0:T(8,128)} async-done(((f32[32,64,512]{2,1,0:T(8,128)}), f32[32,64,512]{2,1,0:T(8,128)}, u32[]{:S(2)}, u32[]{:S(2)}) %all-to-all-start) | async-done | bytes 4194336 | tf_op jit(solution)/shard_map/all_to_all | solution.py:54
  426.9 1.8 slice.24
  428.7 0.0 copy-start.3
  428.7 6.8 fusion.12
  435.5 0.0 copy-done.3
  435.5 4.8 convolution_subtract_fusion
  440.3 386.3 %all-gather.6.cloned.1.call-done = f32[1,1,2048,1024]{3,2,1,0:T(8,128)} async-done(((f32[1,1,64,1024]{3,2,1,0:T(8,128)}), f32[1,1,2048,1024]{3,2,1,0:T(8,128)}) %all-gather.6.cloned.1.call-update) | async-done | bytes 8388624 | tf_op jit(solution)/shard_map/all_gather | solution.py:32
  826.6 16.9 %bitcast_subtract_fusion = f32[512,2048]{1,0:T(8,128)S(1)} fusion(f32[8,1,64,1,1,2048]{5,2,3,4,1,0:T(8,128)} %copy.13, f32[512,1024]{1,0:T(8,128)} %copy-done.2, f32[1,1,2048,1024]{3,2,1,0:T(8,128)} %all-gather.6.cloned.1.call-done), kind=kOutput, calls=%fused_computation.5 | convolution fusion | flops 12885950464 | bytes 18874368 | tf_op jit(solution)/shard_map/rp,cwp->rcw/dot_general | solution.py:29
  843.4 6.3 copy.11
  (7 shorter events, 0.1 us)
Async XLA Ops:
  8.0 81.1 %copy-start = (bf16[1024,1024]{1,0:T(8,128)(2,1)S(1)}, bf16[1024,1024]{1,0:T(8,128)(2,1)}, u32[]{:S(2)}) copy-start(bf16[1024,1024]{1,0:T(8,128)(2,1)} %param.6) | copy-start | bytes 6291460
  8.0 81.1 %all-reduce.2.cloned.1.call-start = ((), (), s32[]{:S(2)}) async-start(), calls=%async_computation.1 | async-start | bytes 4194304 | tf_op jit(solution)/shard_map/psum | solution.py:10
  13.4 0.7 copy-start.1
  13.4 3.0 copy-start.4
  13.4 275.2 %all-gather.4.cloned.1.call-start = ((), (), s32[]{:S(2)}) async-start(), calls=%async_computation.2 | async-start | bytes 4325376 | tf_op jit(solution)/shard_map/all_gather | solution.py:48
  18.0 808.5 %all-gather.6.cloned.1.call-start = ((), (), s32[]{:S(2)}) async-start(), calls=%async_computation.3 | async-start | bytes 8650752 | tf_op jit(solution)/shard_map/all_gather | solution.py:32
  94.1 1.3 copy-start.2
  301.3 125.7 %all-to-all-start = ((f32[32,64,512]{2,1,0:T(8,128)}), f32[32,64,512]{2,1,0:T(8,128)}, u32[]{:S(2)}, u32[]{:S(2)}) async-start(f32[32,64,512]{2,1,0:T(8,128)} %stack.2), calls=%async_computation | async-start | bytes 8388608 | tf_op jit(solution)/shard_map/all_to_all | solution.py:54
  428.7 6.9 copy-start.3
Sparse Core Ops, SparseCore 0:
  13.5 75.4 all-reduce.1
Sparse Core Ops, SparseCore 1:
  18.1 270.4 all-gather.3
  290.3 536.2 all-gather.5
